TPU v7x, 256 devices: a whole 4x4x8 slice. The times are simulated.
256 devices in a mesh: user: 32 (over x_lo, z, core), tensor: 8 (over y, x_hi).
Axes of the slice: x: 4 (x_hi: 2, x_lo: 2; x = x_hi * 2 + x_lo), y: 4, z: 8, core: 2. Of those that a mesh axis runs over, the one named last changes fastest.
Arguments:
- events: bfloat16 [1024, 128, 1024], P('user', None, 'tensor'), may hold values from -6 to 6
- cotangent: bfloat16 [1024, 128, 1024], P('user', None, 'tensor'), may hold values from -6 to 6
- w_in: bfloat16 [1024, 4096], P('user', 'tensor'), may hold values from -0.1875 to 0.1875
- w_out: bfloat16 [1024, 1024], P('user', 'tensor'), may hold values from -0.1875 to 0.1875
- slot_source: int32 [1024], P('user'), may hold values from 0 to 31, as said below
- slot_length: int32 [1024], P('user'), may hold values from 1 to 127, as said below
Outputs:
- grad_x: bfloat16 [1024, 128, 1024], P('user', None, 'tensor')
- grad_w_in: float32 [1024, 4096], P('user', 'tensor')
- grad_w_out: float32 [1024, 1024], P('user', 'tensor')
Inputs may be any that keep to these rules, and one draw needn't show every extreme that they name: `slot_source`: the 32 slots of one host name distinct user shards, and for each slot j the entries h * 32 + j over all hosts h name every user shard once, so every history is placed exactly once. `slot_length`: the 32 slot lengths of one host sum to 2048.
All inputs are finite; a program needn't handle non-finite values.
Results may differ from a plain program's by a relative error of at most 0.023.
Values may be sent and summed in bfloat16 or wider, within the bound.
A program may use at most 128 MiB of HBM per device.

v0:
```python
import math
import jax
import jax.numpy as jnp
from jax import lax
from jax.sharding import PartitionSpec as P

HEAD_DIM = 128
SEQ_LEN = 128
eps = 1e-05


def silu_grad(t):
    sig = jax.nn.sigmoid(t)
    return sig * (1.0 + t * (1.0 - sig))


def host_rows(lengths, sources, total_rows, hist):
    ends = jnp.cumsum(lengths)
    starts = ends - lengths
    rows = jnp.arange(total_rows, dtype=jnp.int32)
    segment = jnp.sum((rows[:, None] >= ends[None, :]).astype(jnp.int32), axis=1)
    onehot = (segment[:, None] == jnp.arange(hist, dtype=jnp.int32)[None, :]).astype(jnp.int32)
    position = rows - jnp.sum(onehot * starts[None, :], axis=1)
    source = jnp.sum(onehot * sources[None, :], axis=1)
    return (segment, position, source, starts)


def local(events, cotangent, w_in, w_out, slot_source, slot_length):
    users = lax.axis_size("user")
    hist, seq_len, width_part = events.shape
    total_rows = hist // 2 * seq_len
    table = lax.all_gather(slot_source, "user", axis=0, tiled=True).reshape(users, hist)
    myself = lax.axis_index("user")
    matches = (table == myself).astype(jnp.int32)
    host_ids = jnp.arange(users, dtype=jnp.int32)[:, None]
    host_of = jnp.sum(matches * host_ids, axis=0)
    send_x = jnp.zeros_like(events).at[host_of].set(events)
    send_d = jnp.zeros_like(cotangent).at[host_of].set(cotangent)
    recv_x, recv_d = (
        lax.all_to_all(send_x, "user", split_axis=0, concat_axis=0, tiled=True),
        lax.all_to_all(send_d, "user", split_axis=0, concat_axis=0, tiled=True),
    )
    segment, position, source, starts = host_rows(slot_length, slot_source, total_rows, hist)
    index = source * seq_len + position
    xp = jnp.take(recv_x.reshape(users * seq_len, width_part), index, axis=0)
    dp = jnp.take(recv_d.reshape(users * seq_len, width_part), index, axis=0)
    x_full, d_full = (
        lax.all_gather(xp, "tensor", axis=1, tiled=True),
        lax.all_gather(dp, "tensor", axis=1, tiled=True),
    )
    w_in_cols = lax.all_gather(w_in, "user", axis=0, tiled=True)
    w_out_cols = lax.all_gather(w_out, "user", axis=0, tiled=True)
    xf = x_full.astype(jnp.float32)
    centred = xf - jnp.mean(xf, axis=1, keepdims=True)
    rstd = lax.rsqrt(jnp.mean(centred * centred, axis=1, keepdims=True) + eps)
    nf = centred * rstd
    nb = nf.astype(jnp.bfloat16)
    z = jnp.dot(nb, w_in_cols, preferred_element_type=jnp.float32)
    local_heads = w_in_cols.shape[1] // (4 * HEAD_DIM)
    g = (
        jax.nn.silu(z)
        .astype(jnp.bfloat16)
        .reshape(total_rows, local_heads, 4, HEAD_DIM)
        .transpose(1, 2, 0, 3)
    )
    upart, vpart, qpart, kpart = (g[:, 0], g[:, 1], g[:, 2], g[:, 3])
    dh = (
        jnp.dot(d_full, w_out_cols, preferred_element_type=jnp.float32)
        .reshape(total_rows, local_heads, HEAD_DIM)
        .transpose(1, 0, 2)
    )
    scale = HEAD_DIM ** (-0.5)
    block = math.gcd(total_rows, 512)
    hparts, grads_u, grads_q = ([], [], [])
    grad_v = jnp.zeros((local_heads, total_rows, HEAD_DIM), jnp.float32)
    grad_k = jnp.zeros((local_heads, total_rows, HEAD_DIM), jnp.float32)
    for number in range(total_rows // block):
        lo = number * block
        hi = lo + block
        mask = (segment[lo:hi, None] == segment[None, :]) & (
            position[None, :] <= position[lo:hi, None]
        )
        q_rows = qpart[:, lo:hi]
        scores = (
            jnp.einsum("hqe,hke->hqk", q_rows, kpart, preferred_element_type=jnp.float32) * scale
        )
        attn = jnp.where(mask[None], jax.nn.silu(scores) / SEQ_LEN, 0.0).astype(jnp.bfloat16)
        yval = jnp.einsum("hqk,hke->hqe", attn, vpart, preferred_element_type=jnp.float32)
        ycen = yval - jnp.mean(yval, axis=2, keepdims=True)
        yrstd = lax.rsqrt(jnp.mean(ycen * ycen, axis=2, keepdims=True) + eps)
        ynorm = ycen * yrstd
        uf = upart[:, lo:hi].astype(jnp.float32)
        hparts.append((ynorm * uf).astype(jnp.bfloat16))
        grad_h = dh[:, lo:hi]
        grads_u.append(grad_h * ynorm)
        grad_yn = grad_h * uf
        grad_y = (
            (
                grad_yn
                - jnp.mean(grad_yn, axis=2, keepdims=True)
                - ynorm * jnp.mean(grad_yn * ynorm, axis=2, keepdims=True)
            )
            * yrstd
        ).astype(jnp.bfloat16)
        grad_a = jnp.einsum("hqe,hke->hqk", grad_y, vpart, preferred_element_type=jnp.float32)
        grad_v = grad_v + jnp.einsum(
            "hqk,hqe->hke", attn, grad_y, preferred_element_type=jnp.float32
        )
        grad_s = jnp.where(mask[None], grad_a * silu_grad(scores) * (scale / SEQ_LEN), 0.0).astype(
            jnp.bfloat16
        )
        grads_q.append(
            jnp.einsum("hqk,hke->hqe", grad_s, kpart, preferred_element_type=jnp.float32)
        )
        grad_k = grad_k + jnp.einsum(
            "hqk,hqe->hke", grad_s, q_rows, preferred_element_type=jnp.float32
        )
    hb = (
        jnp.concatenate(hparts, axis=1)
        .transpose(1, 0, 2)
        .reshape(total_rows, local_heads * HEAD_DIM)
    )
    grad_u = jnp.concatenate(grads_u, axis=1)
    grad_q = jnp.concatenate(grads_q, axis=1)
    dgrad = (
        jnp.stack([grad_u, grad_v, grad_q, grad_k], axis=1)
        .transpose(2, 0, 1, 3)
        .reshape(total_rows, 4 * local_heads * HEAD_DIM)
    )
    dz = (dgrad * silu_grad(z)).astype(jnp.bfloat16)
    columns = d_full
    grad_w_out = lax.psum_scatter(
        lax.dot_general(
            columns, hb, (((0,), (0,)), ((), ())), preferred_element_type=jnp.float32
        ).astype(jnp.bfloat16),
        "user",
        scatter_dimension=0,
        tiled=True,
    ).astype(jnp.float32)
    columns = nb
    grad_w_in = lax.psum_scatter(
        lax.dot_general(
            columns, dz, (((0,), (0,)), ((), ())), preferred_element_type=jnp.float32
        ).astype(jnp.bfloat16),
        "user",
        scatter_dimension=0,
        tiled=True,
    ).astype(jnp.float32)
    dn = lax.dot_general(
        dz, w_in_cols, (((1,), (1,)), ((), ())), preferred_element_type=jnp.float32
    )
    first_col = lax.axis_index("tensor") * width_part
    n_share = lax.dynamic_slice_in_dim(nf, first_col, width_part, 1)
    dn_all = lax.psum(dn, "tensor")
    mean_one = jnp.mean(dn_all, axis=1, keepdims=True)
    mean_two = jnp.mean(dn_all * nf, axis=1, keepdims=True)
    dn_share = lax.dynamic_slice_in_dim(dn_all, first_col, width_part, 1)
    branch = (dn_share - mean_one - n_share * mean_two) * rstd
    dxp = (dp.astype(jnp.float32) + branch).astype(jnp.bfloat16)
    slots = jnp.arange(seq_len, dtype=jnp.int32)
    rows_at = jnp.minimum(starts[:, None] + slots[None, :], total_rows - 1)
    valid = slots[None, :] < slot_length[:, None]
    padded = jnp.take(dxp, rows_at.reshape(-1), axis=0).reshape(hist, seq_len, width_part)
    padded = jnp.where(valid[:, :, None], padded, jnp.zeros_like(padded))
    back = jnp.zeros((users, seq_len, width_part), jnp.bfloat16).at[slot_source].set(padded)
    returned = lax.all_to_all(back, "user", split_axis=0, concat_axis=0, tiled=True)
    grad_x = jnp.take(returned, host_of, axis=0)
    return (grad_x, grad_w_in, grad_w_out)


def solution(mesh):
    in_specs = (
        P("user", None, "tensor"),
        P("user", None, "tensor"),
        P("user", "tensor"),
        P("user", "tensor"),
        P("user"),
        P("user"),
    )
    out_specs = (P("user", None, "tensor"), P("user", "tensor"), P("user", "tensor"))
    return jax.shard_map(local, mesh=mesh, in_specs=in_specs, out_specs=out_specs, check_vma=False)
```

profile of v0, /device:TPU:8, one launch (start us, length us, event | category | flops | bytes accessed | tf_op | source)
XLA Modules:
  0.0 963.1 jit_solution(14565554388155570690)
XLA Ops:
  10.1 19.4 %all-reduce = s32[1024]{0:T(1024)S(1)} all-reduce(s32[1024]{0:T(1024)S(1)} %dynamic-update-slice), channel_id=1, replica_groups=mesh['user'=32,'tensor'=8] {'user'}, use_global_device_ids=true, to_apply=%add | all-reduce | flops 1024 | bytes 8192
  30.8 5.2 scatter_fusion
  36.0 4.1 all-to-all-start
  41.3 4.6 scatter_fusion.1
  45.9 22.5 %all-to-all-done = bf16[32,128,128]{2,1,0:T(8,128)(2,1)S(1)} async-done(((bf16[32,128,128]{2,1,0:T(8,128)(2,1)}), bf16[32,128,128]{2,1,0:T(8,128)(2,1)S(1)}, u32[]{:S(2)}, u32[]{:S(2)}) %all-to-all-start) | async-done | bytes 1048608 | tf_op jit(solution)/shard_map/all_to_all | solution.py:41
  68.5 4.1 all-to-all-start.1
  73.2 6.2 gather_fusion.2
  79.4 21.5 %all-to-all-done.1 = bf16[32,128,128]{2,1,0:T(8,128)(2,1)S(1)} async-done(((bf16[32,128,128]{2,1,0:T(8,128)(2,1)}), bf16[32,128,128]{2,1,0:T(8,128)(2,1)S(1)}, u32[]{:S(2)}, u32[]{:S(2)}) %all-to-all-start.1) | async-done | bytes 1048608 | tf_op jit(solution)/shard_map/all_to_all | solution.py:40
  100.9 6.2 gather_fusion.3
  109.2 36.2 %all_gather.17 = bf16[1024,128]{1,0:T(8,128)(2,1)} all-gather(bf16[32,128]{1,0:T(8,128)(2,1)S(1)} %copy-done.43), channel_id=1, replica_groups=mesh['user'=32,'tensor'=8] {'user'}, dimensions={0}, use_global_device_ids=true | all-gather | bytes 270336 | tf_op jit(solution)/shard_map/all_gather | solution.py:52
  145.9 38.0 %all-gather.6.cloned.1.call-done = bf16[2048,1024]{1,0:T(8,128)(2,1)} async-done(((bf16[2048,128]{1,0:T(8,128)(2,1)}), bf16[2048,1024]{1,0:T(8,128)(2,1)}) %all-gather.6.cloned.1.call-update) | async-done | bytes 4194320 | tf_op jit(solution)/shard_map/all_gather | solution.py:48
  183.9 3.0 convert_reduce_fusion
  188.7 59.8 %all-gather.8.cloned.1.call-done = bf16[1024,512]{1,0:T(8,128)(2,1)} async-done(((bf16[32,512]{1,0:T(8,128)(2,1)}), bf16[1024,512]{1,0:T(8,128)(2,1)}) %all-gather.8.cloned.1.call-update) | async-done | bytes 1048592 | tf_op jit(solution)/shard_map/all_gather | solution.py:51
  248.5 6.9 multiply_convert_fusion
  258.2 8.7 select_convert_fusion.5
  272.5 56.3 %all-gather.4.cloned.1.call-done = bf16[2048,1024]{1,0:T(8,128)(2,1)} async-done(((bf16[2048,128]{1,0:T(8,128)(2,1)}), bf16[2048,1024]{1,0:T(8,128)(2,1)}) %all-gather.4.cloned.1.call-update) | async-done | bytes 4194320 | tf_op jit(solution)/shard_map/all_gather | solution.py:49
  328.8 3.9 convolution_bitcast_fusion
  335.7 3.4 select_convert_fusion.3
  341.6 2.9 select_convert_fusion.2
  346.7 2.9 select_convert_fusion
  353.4 3.1 select_convert_fusion.1
  363.4 5.6 fusion.63
  370.1 4.2 convolution_convert_fusion
  374.4 6.2 fusion.10
  380.6 334.5 %all-reduce.3.cloned.1.call-done = f32[2048,1024]{1,0:T(8,128)} async-done(((f32[2048,1024]{1,0:T(8,128)}), f32[2048,1024]{1,0:T(8,128)}) %all-reduce.3.cloned.1.call-update) | async-done | bytes 8388624 | tf_op jit(solution)/shard_map/psum | solution.py:154
  715.1 6.0 fusion.56
  721.1 2.0 add_convert_fusion
  723.2 12.1 %gather_fusion = bf16[4096,128]{1,0:T(8,128)(2,1)S(1)} fusion(bf16[2048,128]{1,0:T(8,128)(2,1)S(1)} %add_convert_fusion, s32[4096]{0:T(1024)S(1)} %broadcast_clamp_fusion), kind=kCustom, calls=%fused_computation.2 | custom fusion | bytes 2113536 | tf_op jit(solution)/shard_map/jit(_take)/gather | solution.py:163
  738.0 4.6 scatter_fusion.2
  742.6 7.4 all-to-all-start.2
  750.0 85.5 %reduce-scatter.5.cloned.1.call-done = bf16[32,128]{1,0:T(8,128)(2,1)} async-done(((bf16[1024,128]{1,0:T(8,128)(2,1)}), bf16[32,128]{1,0:T(8,128)(2,1)}) %reduce-scatter.5.cloned.1.call-update) | async-done | bytes 8208 | tf_op jit(solution)/shard_map/reduce_scatter | solution.py:132
  836.8 115.9 %reduce-scatter.3.cloned.1.call-done = bf16[32,512]{1,0:T(8,128)(2,1)} async-done(((bf16[1024,512]{1,0:T(8,128)(2,1)}), bf16[32,512]{1,0:T(8,128)(2,1)}) %reduce-scatter.3.cloned.1.call-update) | async-done | bytes 32784 | tf_op jit(solution)/shard_map/reduce_scatter | solution.py:141
  (242 shorter events, 43.9 us)
Async XLA Ops:
  7.2 34.2 %copy-start.23 = (bf16[32,128,128]{2,1,0:T(8,128)(2,1)S(1)}, bf16[32,128,128]{2,1,0:T(8,128)(2,1)}, u32[]{:S(2)}) copy-start(bf16[32,128,128]{2,1,0:T(8,128)(2,1)} %param.8) | copy-start | bytes 3145732
  36.0 36.6 %copy-start.64 = (s32[32]{0:T(128)S(1)}, s32[32]{0:T(128)}, u32[]{:S(2)}) copy-start(s32[32]{0:T(128)} %param.13) | copy-start | bytes 388
  36.0 37.0 %copy-start.66 = (s32[32]{0:T(128)S(1)}, s32[32]{0:T(128)}, u32[]{:S(2)}) copy-start(s32[32]{0:T(128)} %param.12) | copy-start | bytes 388
  36.0 32.4 %all-to-all-start = ((bf16[32,128,128]{2,1,0:T(8,128)(2,1)}), bf16[32,128,128]{2,1,0:T(8,128)(2,1)S(1)}, u32[]{:S(2)}, u32[]{:S(2)}) async-start(bf16[32,128,128]{2,1,0:T(8,128)(2,1)} %scatter_fusion), calls=%async_computation | async-start | bytes 2097152 | tf_op jit(solution)/shard_map/all_to_all | solution.py:41
  68.5 32.5 %all-to-all-start.1 = ((bf16[32,128,128]{2,1,0:T(8,128)(2,1)}), bf16[32,128,128]{2,1,0:T(8,128)(2,1)S(1)}, u32[]{:S(2)}, u32[]{:S(2)}) async-start(bf16[32,128,128]{2,1,0:T(8,128)(2,1)} %scatter_fusion.1), calls=%async_computation.1 | async-start | bytes 2097152 | tf_op jit(solution)/shard_map/all_to_all | solution.py:40
  72.6 111.3 %all-gather.6.cloned.1.call-start = ((), (), s32[]{:S(2)}) async-start(), calls=%async_computation.6 | async-start | bytes 4718592 | tf_op jit(solution)/shard_map/all_gather | solution.py:48
  72.9 34.2 %copy-start.44 = (s32[32]{0:T(128)}, s32[32]{0:T(128)S(1)}, u32[]{:S(2)}) copy-start(s32[32]{0:T(128)S(1)} %sub.128) | copy-start | bytes 388
  73.0 184.7 %copy-start.27 = (s32[2048]{0:T(1024)}, s32[2048]{0:T(1024)S(1)}, u32[]{:S(2)}) copy-start(s32[2048]{0:T(1024)S(1)} %convert_reduce_fusion.1) | copy-start | bytes 24580
  73.2 184.5 %copy-start.41 = (s32[2048]{0:T(1024)}, s32[2048]{0:T(1024)S(1)}, u32[]{:S(2)}) copy-start(s32[2048]{0:T(1024)S(1)} %get-tuple-element.43) | copy-start | bytes 24580
  108.4 140.1 %all-gather.8.cloned.1.call-start = ((), (), s32[]{:S(2)}) async-start(), calls=%async_computation.7 | async-start | bytes 1081344 | tf_op jit(solution)/shard_map/all_gather | solution.py:51
  109.2 219.7 %all-gather.4.cloned.1.call-start = ((), (), s32[]{:S(2)}) async-start(), calls=%async_computation.5 | async-start | bytes 4718592 | tf_op jit(solution)/shard_map/all_gather | solution.py:49
  145.5 112.3 %copy-start.48 = (s32[512]{0:T(512)}, s32[512]{0:T(512)S(1)}, u32[]{:S(2)}) copy-start(s32[512]{0:T(512)S(1)} %get-tuple-element.35) | copy-start | bytes 6148
  145.5 112.3 %copy-start.50 = (s32[512]{0:T(512)}, s32[512]{0:T(512)S(1)}, u32[]{:S(2)}) copy-start(s32[512]{0:T(512)S(1)} %get-tuple-element.61) | copy-start | bytes 6148
  145.5 112.3 %copy-start.52 = (s32[512]{0:T(512)}, s32[512]{0:T(512)S(1)}, u32[]{:S(2)}) copy-start(s32[512]{0:T(512)S(1)} %get-tuple-element.36) | copy-start | bytes 6148
  145.5 112.3 %copy-start.54 = (s32[512]{0:T(512)}, s32[512]{0:T(512)S(1)}, u32[]{:S(2)}) copy-start(s32[512]{0:T(512)S(1)} %get-tuple-element.60) | copy-start | bytes 6148
  145.5 112.3 %copy-start.56 = (s32[512]{0:T(512)}, s32[512]{0:T(512)S(1)}, u32[]{:S(2)}) copy-start(s32[512]{0:T(512)S(1)} %get-tuple-element.37) | copy-start | bytes 6148
  145.5 112.3 %copy-start.58 = (s32[512]{0:T(512)}, s32[512]{0:T(512)S(1)}, u32[]{:S(2)}) copy-start(s32[512]{0:T(512)S(1)} %get-tuple-element.59) | copy-start | bytes 6148
  145.5 112.3 %copy-start.60 = (s32[512]{0:T(512)}, s32[512]{0:T(512)S(1)}, u32[]{:S(2)}) copy-start(s32[512]{0:T(512)S(1)} %get-tuple-element.38) | copy-start | bytes 6148
  145.5 112.3 %copy-start.62 = (s32[512]{0:T(512)}, s32[512]{0:T(512)S(1)}, u32[]{:S(2)}) copy-start(s32[512]{0:T(512)S(1)} %get-tuple-element.58) | copy-start | bytes 6148
  145.5 569.6 %all-reduce.3.cloned.1.call-start = ((), (), s32[]{:S(2)}) async-start(), calls=%async_computation.8 | async-start | bytes 16777216 | tf_op jit(solution)/shard_map/psum | solution.py:154
  267.8 64.9 %copy-start.37 = (f32[512]{0:T(512)}, f32[512]{0:T(512)S(1)}, u32[]{:S(2)}) copy-start(f32[512]{0:T(512)S(1)} %broadcast_multiply_fusion.14) | copy-start | bytes 6148
  268.7 64.2 %copy-start.29 = (f32[512]{0:T(512)}, f32[512]{0:T(512)S(1)}, u32[]{:S(2)}) copy-start(f32[512]{0:T(512)S(1)} %broadcast_multiply_fusion.13) | copy-start | bytes 6148
  270.1 62.9 %copy-start.31 = (f32[512]{0:T(512)}, f32[512]{0:T(512)S(1)}, u32[]{:S(2)}) copy-start(f32[512]{0:T(512)S(1)} %broadcast_multiply_fusion.12) | copy-start | bytes 6148
  271.7 61.6 %copy-start.38 = (f32[512]{0:T(512)}, f32[512]{0:T(512)S(1)}, u32[]{:S(2)}) copy-start(f32[512]{0:T(512)S(1)} %broadcast_multiply_fusion.11) | copy-start | bytes 6148
  272.4 60.8 %copy-start.39 = (f32[512]{0:T(512)}, f32[512]{0:T(512)S(1)}, u32[]{:S(2)}) copy-start(f32[512]{0:T(512)S(1)} %add_rsqrt_fusion.4) | copy-start | bytes 6148
  272.5 60.8 %copy-start.33 = (f32[512]{0:T(512)}, f32[512]{0:T(512)S(1)}, u32[]{:S(2)}) copy-start(f32[512]{0:T(512)S(1)} %add_rsqrt_fusion.3) | copy-start | bytes 6148
  272.5 60.8 %copy-start.35 = (f32[512]{0:T(512)}, f32[512]{0:T(512)S(1)}, u32[]{:S(2)}) copy-start(f32[512]{0:T(512)S(1)} %add_rsqrt_fusion.2) | copy-start | bytes 6148
  272.5 60.8 %copy-start.40 = (f32[512]{0:T(512)}, f32[512]{0:T(512)S(1)}, u32[]{:S(2)}) copy-start(f32[512]{0:T(512)S(1)} %add_rsqrt_fusion.1) | copy-start | bytes 6148
  369.1 466.4 %reduce-scatter.5.cloned.1.call-start = ((), (), s32[]{:S(2)}) async-start(), calls=%async_computation.10 | async-start | bytes 270336 | tf_op jit(solution)/shard_map/reduce_scatter | solution.py:132
  374.3 578.4 %reduce-scatter.3.cloned.1.call-start = ((), (), s32[]{:S(2)}) async-start(), calls=%async_computation.9 | async-start | bytes 1081344 | tf_op jit(solution)/shard_map/reduce_scatter | solution.py:141
  380.6 340.5 %copy-start.1 = (bf16[2048,128]{1,0:T(8,128)(2,1)S(1)}, bf16[2048,128]{1,0:T(8,128)(2,1)}, u32[]{:S(2)}) copy-start(bf16[2048,128]{1,0:T(8,128)(2,1)} %get-tuple-element.45) | copy-start | bytes 1572868
  742.6 211.6 %all-to-all-start.2 = ((bf16[32,128,128]{2,1,0:T(8,128)(2,1)}), bf16[32,128,128]{2,1,0:T(8,128)(2,1)S(1)}, u32[]{:S(2)}, u32[]{:S(2)}) async-start(bf16[32,128,128]{2,1,0:T(8,128)(2,1)} %scatter_fusion.2), calls=%async_computation.2 | async-start | bytes 2097152 | tf_op jit(solution)/shard_map/all_to_all | solution.py:166
  (49 other events, 200.4 us)
Sparse Core Ops, SparseCore 0:
  108.5 75.2 all-gather.5
  185.7 62.7 all-gather.7
  251.6 77.1 all-gather.3
  369.2 345.8 all-reduce.2
  717.5 118.0 reduce-scatter.4
  838.0 114.6 reduce-scatter.2
where the time goes:
time: 968 us; the launch traced here: 963 us
  waiting for transfers between devices  735 us (76%)
  matrix products  60.5 us (6%)
  blocking collectives  55.6 us (6%)
  local copies, waits for them, and re-layouts  54.9 us (6%)
  other arithmetic  24.9 us (3%)
  between operations  16.3 us (2%)
  starting transfers between devices  16.1 us (2%)
    psum x1, waiting for transfers between devices, local(): dn_all = lax.psum(dn, 'tensor')  334 us
    reduce_scatter x1, waiting for transfers between devices, local(): lax.psum_scatter(lax.dot_general(columns, dz, (((0,), (0,)), ((), ())), p...  116 us
    reduce_scatter x1, waiting for transfers between devices, local(): lax.psum_scatter(lax.dot_general(columns, hb, (((0,), (0,)), ((), ())), p...  85.5 us
    all_gather x1, waiting for transfers between devices, local(): w_in_cols = lax.all_gather(w_in, 'user', axis=0, tiled=True)  59.8 us
    all_gather x1, waiting for transfers between devices, local(): lax.all_gather(dp, 'tensor', axis=1, tiled=True)  56.3 us
    all_gather x1, waiting for transfers between devices, local(): lax.all_gather(xp, 'tensor', axis=1, tiled=True)  38 us
    all_gather x1, blocking collectives, local(): w_out_cols = lax.all_gather(w_out, 'user', axis=0, tiled=True)  36.2 us
    all_to_all x1, waiting for transfers between devices, local(): lax.all_to_all(send_d, 'user', split_axis=0, concat_axis=0, tiled=True)  22.5 us
  transfers between devices with their start and end apart: 9, of which 8 were waited for; matrix products, arithmetic and copies ran while one was open for 8% of the time, Pallas kernels for 0%

commit v1 on v0

--- a/solution.py
+++ b/solution.py
@@ -151,7 +151,7 @@
     )
     first_col = lax.axis_index("tensor") * width_part
     n_share = lax.dynamic_slice_in_dim(nf, first_col, width_part, 1)
-    dn_all = lax.psum(dn, "tensor")
+    dn_all = jnp.sum(lax.all_gather(dn, "tensor"), axis=0)
     mean_one = jnp.mean(dn_all, axis=1, keepdims=True)
     mean_two = jnp.mean(dn_all * nf, axis=1, keepdims=True)
     dn_share = lax.dynamic_slice_in_dim(dn_all, first_col, width_part, 1)

time: 968 us -> 1260 us (1.30)
  waiting for transfers between devices: 735 us -> 984 us
  other arithmetic: 24.9 us -> 69.8 us
    all_gather x0 -> x1, waiting for transfers between devices: none -> 628 us  [local(): dn_all = jnp.sum(lax.all_gather(dn, 'tensor'), axis=0)]
    psum x1 -> x0, waiting for transfers between devices: 334 us -> none  [local(): dn_all = lax.psum(dn, 'tensor')]
    reduce_scatter x1, waiting for transfers between devices: 85.5 us -> 39.5 us  [local(): lax.psum_scatter(lax.dot_general(columns, hb, (((0,), (0,)), ((), ())), p...]
    reduce_sum x0 -> x2, other arithmetic: none -> 30.3 us  [the longest x1 24.6 us: local(): dn_all = jnp.sum(lax.all_gather(dn, 'tensor'), axis=0)]
    reduce_sum x1 -> x2, other arithmetic: 5.99 us -> 20.8 us  [local(): mean_one = jnp.mean(dn_all, axis=1, keepdims=True)]
  transfers between devices with their start and end apart: 9 -> 9, of which waited for: 8 -> 8; matrix products, arithmetic and copies ran while one was open for 8% -> 10% of each run, Pallas kernels for 0% -> 0%
where the time goes in v1:
time: 1260 us
  waiting for transfers between devices  984 us (78%)
  other arithmetic  69.8 us (6%)
  matrix products  60.4 us (5%)
  blocking collectives  55.6 us (4%)
  local copies, waits for them, and re-layouts  54.3 us (4%)
  starting transfers between devices  16.4 us (1%)
  between operations  16.2 us (1%)
    all_gather x1, waiting for transfers between devices, local(): dn_all = jnp.sum(lax.all_gather(dn, 'tensor'), axis=0)  628 us
    reduce_scatter x1, waiting for transfers between devices, local(): lax.psum_scatter(lax.dot_general(columns, dz, (((0,), (0,)), ((), ())), p...  116 us
    all_gather x1, waiting for transfers between devices, local(): w_in_cols = lax.all_gather(w_in, 'user', axis=0, tiled=True)  59.8 us
    all_gather x1, waiting for transfers between devices, local(): lax.all_gather(dp, 'tensor', axis=1, tiled=True)  57.6 us
    reduce_scatter x1, waiting for transfers between devices, local(): lax.psum_scatter(lax.dot_general(columns, hb, (((0,), (0,)), ((), ())), p...  39.5 us
    all_gather x1, waiting for transfers between devices, local(): lax.all_gather(xp, 'tensor', axis=1, tiled=True)  38 us
    all_gather x1, blocking collectives, local(): w_out_cols = lax.all_gather(w_out, 'user', axis=0, tiled=True)  36.2 us
  transfers between devices with their start and end apart: 9, of which 8 were waited for; matrix products, arithmetic and copies ran while one was open for 10% of the time, Pallas kernels for 0%

profile of v1, /device:TPU:8, one launch (start us, length us, event | category | flops | bytes accessed | tf_op | source)
XLA Modules:
  0.0 1256.9 jit_solution(17807620799596039650)
XLA Ops:
  10.1 19.4 %all-reduce = s32[1024]{0:T(1024)S(1)} all-reduce(s32[1024]{0:T(1024)S(1)} %dynamic-update-slice), channel_id=1, replica_groups=mesh['user'=32,'tensor'=8] {'user'}, use_global_device_ids=true, to_apply=%add | all-reduce | flops 1024 | bytes 8192
  30.8 5.3 scatter_fusion.1
  36.1 4.1 all-to-all-start.1
  41.3 4.6 scatter_fusion
  45.9 22.6 %all-to-all-done.1 = bf16[32,128,128]{2,1,0:T(8,128)(2,1)S(1)} async-done(((bf16[32,128,128]{2,1,0:T(8,128)(2,1)}), bf16[32,128,128]{2,1,0:T(8,128)(2,1)S(1)}, u32[]{:S(2)}, u32[]{:S(2)}) %all-to-all-start.1) | async-done | bytes 1048608 | tf_op jit(solution)/shard_map/all_to_all | solution.py:40
  68.5 4.1 all-to-all-start
  73.3 6.2 gather_fusion.3
  79.5 21.5 %all-to-all-done = bf16[32,128,128]{2,1,0:T(8,128)(2,1)S(1)} async-done(((bf16[32,128,128]{2,1,0:T(8,128)(2,1)}), bf16[32,128,128]{2,1,0:T(8,128)(2,1)S(1)}, u32[]{:S(2)}, u32[]{:S(2)}) %all-to-all-start) | async-done | bytes 1048608 | tf_op jit(solution)/shard_map/all_to_all | solution.py:41
  101.0 6.2 gather_fusion.2
  109.2 36.2 %all_gather.23 = bf16[1024,128]{1,0:T(8,128)(2,1)} all-gather(bf16[32,128]{1,0:T(8,128)(2,1)S(1)} %copy-done.36), channel_id=1, replica_groups=mesh['user'=32,'tensor'=8] {'user'}, dimensions={0}, use_global_device_ids=true | all-gather | bytes 270336 | tf_op jit(solution)/shard_map/all_gather | solution.py:52
  145.9 38.0 %all-gather.8.cloned.1.call-done = bf16[2048,1024]{1,0:T(8,128)(2,1)} async-done(((bf16[2048,128]{1,0:T(8,128)(2,1)}), bf16[2048,1024]{1,0:T(8,128)(2,1)}) %all-gather.8.cloned.1.call-update) | async-done | bytes 4194320 | tf_op jit(solution)/shard_map/all_gather | solution.py:48
  183.9 3.0 convert_reduce_fusion
  188.7 59.8 %all-gather.10.cloned.1.call-done = bf16[1024,512]{1,0:T(8,128)(2,1)} async-done(((bf16[32,512]{1,0:T(8,128)(2,1)}), bf16[1024,512]{1,0:T(8,128)(2,1)}) %all-gather.10.cloned.1.call-update) | async-done | bytes 1048592 | tf_op jit(solution)/shard_map/all_gather | solution.py:51
  248.5 6.9 multiply_convert_fusion
  258.2 8.6 select_convert_fusion.5
  271.3 57.6 %all-gather.6.cloned.1.call-done = bf16[2048,1024]{1,0:T(8,128)(2,1)} async-done(((bf16[2048,128]{1,0:T(8,128)(2,1)}), bf16[2048,1024]{1,0:T(8,128)(2,1)}) %all-gather.6.cloned.1.call-update) | async-done | bytes 4194320 | tf_op jit(solution)/shard_map/all_gather | solution.py:49
  328.8 3.9 convolution_bitcast_fusion
  335.9 3.4 select_convert_fusion.3
  341.6 2.9 select_convert_fusion
  350.6 3.1 select_convert_fusion.1
  363.6 5.6 fusion.62
  370.2 4.2 convolution_convert_fusion
  374.7 6.3 fusion.10
  381.0 628.2 %all-gather.12.cloned.1.call-done = f32[16384,1024]{1,0:T(8,128)} async-done(((f32[2048,1024]{1,0:T(8,128)}), f32[16384,1024]{1,0:T(8,128)}) %all-gather.12.cloned.1.call-update) | async-done | bytes 67108880 | tf_op jit(solution)/shard_map/all_gather | solution.py:154
  1009.2 24.6 %reduce_sum.250 = f32[2048,1024]{1,0:T(8,128)} reduce(f32[8,2048,1024]{2,1,0:T(8,128)} %bitcast.40, f32[]{:T(128)} %constant.104.clone.1), dimensions={0}, to_apply=%region_25.27 | reduce | flops 14680064 | bytes 75497472 | tf_op jit(solution)/shard_map/reduce_sum | solution.py:154
  1033.8 20.8 %reduce.25 = f32[16384]{0:T(1024)S(1)} reduce(f32[16384,1024]{1,0:T(8,128)} %all-gather.12.cloned.1.call-done, f32[]{:T(128)} %constant.104.clone.1), dimensions={1}, to_apply=%region_26.28 | reduce | flops 16760832 | bytes 67174400 | tf_op jit(solution)/shard_map/reduce_sum | solution.py:155
  1054.7 5.6 multiply_reduce_fusion
  1062.4 12.1 gather_fusion
  1077.2 4.6 scatter_fusion.2
  1081.8 7.5 all-to-all-start.2
  1089.4 39.5 %reduce-scatter.5.cloned.1.call-done = bf16[32,128]{1,0:T(8,128)(2,1)} async-done(((bf16[1024,128]{1,0:T(8,128)(2,1)}), bf16[32,128]{1,0:T(8,128)(2,1)}) %reduce-scatter.5.cloned.1.call-update) | async-done | bytes 8208 | tf_op jit(solution)/shard_map/reduce_scatter | solution.py:132
  1130.2 116.4 %reduce-scatter.3.cloned.1.call-done = bf16[32,512]{1,0:T(8,128)(2,1)} async-done(((bf16[1024,512]{1,0:T(8,128)(2,1)}), bf16[32,512]{1,0:T(8,128)(2,1)}) %reduce-scatter.3.cloned.1.call-update) | async-done | bytes 32784 | tf_op jit(solution)/shard_map/reduce_scatter | solution.py:141
  (232 shorter events, 48.2 us)
Async XLA Ops:
  7.2 34.2 %copy-start.20 = (bf16[32,128,128]{2,1,0:T(8,128)(2,1)S(1)}, bf16[32,128,128]{2,1,0:T(8,128)(2,1)}, u32[]{:S(2)}) copy-start(bf16[32,128,128]{2,1,0:T(8,128)(2,1)} %param.9) | copy-start | bytes 3145732
  29.6 16.3 %copy-start.39 = (s32[32]{0:T(128)}, s32[32]{0:T(128)S(1)}, u32[]{:S(2)}) copy-start(s32[32]{0:T(128)S(1)} %fusion.52) | copy-start | bytes 388
  36.0 36.6 %copy-start.57 = (s32[32]{0:T(128)S(1)}, s32[32]{0:T(128)}, u32[]{:S(2)}) copy-start(s32[32]{0:T(128)} %param.13) | copy-start | bytes 388
  36.0 37.0 %copy-start.59 = (s32[32]{0:T(128)S(1)}, s32[32]{0:T(128)}, u32[]{:S(2)}) copy-start(s32[32]{0:T(128)} %param.12) | copy-start | bytes 388
  36.1 32.4 %all-to-all-start.1 = ((bf16[32,128,128]{2,1,0:T(8,128)(2,1)}), bf16[32,128,128]{2,1,0:T(8,128)(2,1)S(1)}, u32[]{:S(2)}, u32[]{:S(2)}) async-start(bf16[32,128,128]{2,1,0:T(8,128)(2,1)} %scatter_fusion.1), calls=%async_computation.1 | async-start | bytes 2097152 | tf_op jit(solution)/shard_map/all_to_all | solution.py:40
  68.5 32.5 %all-to-all-start = ((bf16[32,128,128]{2,1,0:T(8,128)(2,1)}), bf16[32,128,128]{2,1,0:T(8,128)(2,1)S(1)}, u32[]{:S(2)}, u32[]{:S(2)}) async-start(bf16[32,128,128]{2,1,0:T(8,128)(2,1)} %scatter_fusion), calls=%async_computation | async-start | bytes 2097152 | tf_op jit(solution)/shard_map/all_to_all | solution.py:41
  72.6 111.3 %all-gather.8.cloned.1.call-start = ((), (), s32[]{:S(2)}) async-start(), calls=%async_computation.6 | async-start | bytes 4718592 | tf_op jit(solution)/shard_map/all_gather | solution.py:48
  72.9 34.2 %copy-start.37 = (s32[32]{0:T(128)}, s32[32]{0:T(128)S(1)}, u32[]{:S(2)}) copy-start(s32[32]{0:T(128)S(1)} %sub.128) | copy-start | bytes 388
  73.0 184.7 %copy-start.24 = (s32[2048]{0:T(1024)}, s32[2048]{0:T(1024)S(1)}, u32[]{:S(2)}) copy-start(s32[2048]{0:T(1024)S(1)} %convert_reduce_fusion.1) | copy-start | bytes 24580
  73.2 184.5 %copy-start.34 = (s32[2048]{0:T(1024)}, s32[2048]{0:T(1024)S(1)}, u32[]{:S(2)}) copy-start(s32[2048]{0:T(1024)S(1)} %get-tuple-element.42) | copy-start | bytes 24580
  79.4 29.8 %copy-start.36 = (bf16[32,128]{1,0:T(8,128)(2,1)S(1)}, bf16[32,128]{1,0:T(8,128)(2,1)}, u32[]{:S(2)}) copy-start(bf16[32,128]{1,0:T(8,128)(2,1)} %param.11) | copy-start | bytes 24580
  108.4 140.1 %all-gather.10.cloned.1.call-start = ((), (), s32[]{:S(2)}) async-start(), calls=%async_computation.7 | async-start | bytes 1081344 | tf_op jit(solution)/shard_map/all_gather | solution.py:51
  109.2 219.7 %all-gather.6.cloned.1.call-start = ((), (), s32[]{:S(2)}) async-start(), calls=%async_computation.5 | async-start | bytes 4718592 | tf_op jit(solution)/shard_map/all_gather | solution.py:49
  145.4 112.3 %copy-start.41 = (s32[512]{0:T(512)}, s32[512]{0:T(512)S(1)}, u32[]{:S(2)}) copy-start(s32[512]{0:T(512)S(1)} %get-tuple-element.34) | copy-start | bytes 6148
  145.4 112.3 %copy-start.43 = (s32[512]{0:T(512)}, s32[512]{0:T(512)S(1)}, u32[]{:S(2)}) copy-start(s32[512]{0:T(512)S(1)} %get-tuple-element.60) | copy-start | bytes 6148
  145.4 112.3 %copy-start.45 = (s32[512]{0:T(512)}, s32[512]{0:T(512)S(1)}, u32[]{:S(2)}) copy-start(s32[512]{0:T(512)S(1)} %get-tuple-element.36) | copy-start | bytes 6148
  145.5 112.3 %copy-start.47 = (s32[512]{0:T(512)}, s32[512]{0:T(512)S(1)}, u32[]{:S(2)}) copy-start(s32[512]{0:T(512)S(1)} %get-tuple-element.58) | copy-start | bytes 6148
  145.5 112.3 %copy-start.49 = (s32[512]{0:T(512)}, s32[512]{0:T(512)S(1)}, u32[]{:S(2)}) copy-start(s32[512]{0:T(512)S(1)} %get-tuple-element.35) | copy-start | bytes 6148
  145.5 112.3 %copy-start.51 = (s32[512]{0:T(512)}, s32[512]{0:T(512)S(1)}, u32[]{:S(2)}) copy-start(s32[512]{0:T(512)S(1)} %get-tuple-element.59) | copy-start | bytes 6148
  145.5 112.3 %copy-start.53 = (s32[512]{0:T(512)}, s32[512]{0:T(512)S(1)}, u32[]{:S(2)}) copy-start(s32[512]{0:T(512)S(1)} %get-tuple-element.37) | copy-start | bytes 6148
  145.5 112.3 %copy-start.55 = (s32[512]{0:T(512)}, s32[512]{0:T(512)S(1)}, u32[]{:S(2)}) copy-start(s32[512]{0:T(512)S(1)} %get-tuple-element.57) | copy-start | bytes 6148
  145.5 863.7 %all-gather.12.cloned.1.call-start = ((), (), s32[]{:S(2)}) async-start(), calls=%async_computation.10 | async-start | bytes 75497472 | tf_op jit(solution)/shard_map/all_gather | solution.py:154
  267.7 66.2 %copy-start.26 = (f32[512]{0:T(512)}, f32[512]{0:T(512)S(1)}, u32[]{:S(2)}) copy-start(f32[512]{0:T(512)S(1)} %broadcast_multiply_fusion.12) | copy-start | bytes 6148
  268.6 65.3 %copy-start.30 = (f32[512]{0:T(512)}, f32[512]{0:T(512)S(1)}, u32[]{:S(2)}) copy-start(f32[512]{0:T(512)S(1)} %broadcast_multiply_fusion.11) | copy-start | bytes 6148
  270.5 63.3 %copy-start.31 = (f32[512]{0:T(512)}, f32[512]{0:T(512)S(1)}, u32[]{:S(2)}) copy-start(f32[512]{0:T(512)S(1)} %broadcast_multiply_fusion.14) | copy-start | bytes 6148
  271.2 62.7 %copy-start.28 = (f32[512]{0:T(512)}, f32[512]{0:T(512)S(1)}, u32[]{:S(2)}) copy-start(f32[512]{0:T(512)S(1)} %add_rsqrt_fusion.2) | copy-start | bytes 6148
  271.2 62.7 %copy-start.32 = (f32[512]{0:T(512)}, f32[512]{0:T(512)S(1)}, u32[]{:S(2)}) copy-start(f32[512]{0:T(512)S(1)} %add_rsqrt_fusion.1) | copy-start | bytes 6148
  271.2 62.5 %copy-start.33 = (f32[512]{0:T(512)}, f32[512]{0:T(512)S(1)}, u32[]{:S(2)}) copy-start(f32[512]{0:T(512)S(1)} %add_rsqrt_fusion.4) | copy-start | bytes 6148
  369.2 759.7 %reduce-scatter.5.cloned.1.call-start = ((), (), s32[]{:S(2)}) async-start(), calls=%async_computation.9 | async-start | bytes 270336 | tf_op jit(solution)/shard_map/reduce_scatter | solution.py:132
  374.5 872.1 %reduce-scatter.3.cloned.1.call-start = ((), (), s32[]{:S(2)}) async-start(), calls=%async_computation.8 | async-start | bytes 1081344 | tf_op jit(solution)/shard_map/reduce_scatter | solution.py:141
  1074.6 14.8 %copy-start.62 = (s32[32]{0:T(128)S(1)}, s32[32]{0:T(128)}, u32[]{:S(2)}) copy-start(s32[32]{0:T(128)} %copy-done.61) | copy-start | bytes 388
  1081.8 166.2 %all-to-all-start.2 = ((bf16[32,128,128]{2,1,0:T(8,128)(2,1)}), bf16[32,128,128]{2,1,0:T(8,128)(2,1)S(1)}, u32[]{:S(2)}, u32[]{:S(2)}) async-start(bf16[32,128,128]{2,1,0:T(8,128)(2,1)} %scatter_fusion.2), calls=%async_computation.2 | async-start | bytes 2097152 | tf_op jit(solution)/shard_map/all_to_all | solution.py:166
  (42 other events, 137.5 us)
Sparse Core Ops, SparseCore 0:
  108.5 75.2 all-gather.7
  185.7 62.7 all-gather.9
  251.6 77.1 all-gather.5
  369.4 639.7 all-gather.11
  1011.5 117.3 reduce-scatter.4
  1131.4 115.1 reduce-scatter.2
